TPU v7x, 256 devices: a whole 4x4x8 slice. The times are simulated.
256 devices in a mesh: outer: 64 (over x_hi, z, y), inner: 4 (over x_lo, core).
Axes of the slice: x: 4 (x_hi: 2, x_lo: 2; x = x_hi * 2 + x_lo), y: 4, z: 8, core: 2. Of those that a mesh axis runs over, the one named last changes fastest.
Arguments:
- queries: bfloat16 [65536, 1536], P(('outer', 'inner')), may hold values from -8 to 8
- key_rows: bfloat16 [65536, 1536], P(('outer', 'inner')), may hold values from -8 to 8
- value_rows: bfloat16 [65536, 1536], P(('outer', 'inner')), may hold values from -6 to 6
- upstream: bfloat16 [65536, 1536], P(('outer', 'inner')), may hold values from -6 to 6
- short_offsets: int32 [16], replicated, may hold values from 0 to 1
- global_offsets: int32 [16], replicated, may hold values from 0 to 127
Outputs:
- grad_queries: bfloat16 [65536, 1536], P(('outer', 'inner'))
- grad_keys: bfloat16 [65536, 1536], P(('outer', 'inner'))
- grad_values: bfloat16 [65536, 1536], P(('outer', 'inner'))
All inputs are finite; a program needn't handle non-finite values.
Results may differ from a plain program's by a relative error of at most 0.006.
The roundings to bfloat16 on the way count: a program that leaves them out, or rounds other values in their place, can miss the bound.
Values may be sent and summed in bfloat16 or wider, within the bound.
No kernel may reach another device: no remote copies, remote signals or barrier semaphores. Data moves between devices by JAX's collectives and lax.ppermute only.
A program may use at most 128 MiB of HBM per device.

v0:
```python
import jax
import jax.numpy as jnp
from jax import lax
from jax.sharding import PartitionSpec as P

H = 16
HD = 96
D = 1536
TOK_DEV = 256
KEEP_A = 512
KEEP_B = 512


def pick_rows(block, offsets, stride):
    count = block.shape[0] // stride
    shaped = block.reshape(count, stride, H, HD)
    onehot = (jnp.arange(stride, dtype=jnp.int32)[:, None] == offsets[None, :]).astype(block.dtype)
    return jnp.sum(shaped * onehot[None, :, :, None], axis=1)


def put_rows(grads, offsets, stride):
    onehot = (jnp.arange(stride, dtype=jnp.int32)[:, None] == offsets[None, :]).astype(jnp.float32)
    spread = grads[:, None, :, :] * onehot[None, :, :, None]
    return spread.reshape(grads.shape[0] * stride, H * HD)


def as_heads(flat):
    return flat.reshape(flat.shape[0], H, HD)


def attend_back(query_part, key_part, value_part, grad_part):
    softmax_scale = HD ** (-0.5)
    scores = (
        jnp.einsum("qhd,khd->hqk", query_part, key_part, preferred_element_type=jnp.float32)
        * softmax_scale
    )
    row_max = jnp.max(scores, axis=-1, keepdims=True)
    weights = jnp.exp(scores - row_max)
    probs = weights / jnp.sum(weights, axis=-1, keepdims=True)
    probs_low = probs.astype(jnp.bfloat16)
    output = jnp.einsum("hqk,khd->qhd", probs_low, value_part, preferred_element_type=jnp.float32)
    delta = jnp.sum(grad_part.astype(jnp.float32) * output, axis=-1)
    dprobs = jnp.einsum("qhd,khd->hqk", grad_part, value_part, preferred_element_type=jnp.float32)
    dscores = (probs * (dprobs - jnp.transpose(delta)[:, :, None])).astype(jnp.bfloat16)
    grad_q = (
        jnp.einsum("hqk,khd->qhd", dscores, key_part, preferred_element_type=jnp.float32)
        * softmax_scale
    )
    grad_k = (
        jnp.einsum("hqk,qhd->khd", dscores, query_part, preferred_element_type=jnp.float32)
        * softmax_scale
    )
    grad_v = jnp.einsum("hqk,qhd->khd", probs_low, grad_part, preferred_element_type=jnp.float32)
    return (grad_q, grad_k, grad_v)


def grouped_back(query_part, key_part, value_part, grad_part):
    head_groups = 4

    def split_heads(member):
        return jnp.moveaxis(
            member.reshape(member.shape[0], head_groups, H // head_groups, HD), 1, 0
        )

    def single_group(pack):
        return attend_back(pack[0], pack[1], pack[2], pack[3])

    mapped = lax.map(
        single_group,
        (
            split_heads(query_part),
            split_heads(key_part),
            split_heads(value_part),
            split_heads(grad_part),
        ),
    )
    return [jnp.moveaxis(member, 0, 1).reshape(member.shape[1], H, HD) for member in mapped]


def local(queries, key_rows, value_rows, upstream, short_offsets, global_offsets):
    inner_size = lax.axis_size("inner")
    all_size = lax.axis_size(("outer", "inner"))
    short_stride = TOK_DEV * inner_size // KEEP_A
    far_count = KEEP_B // all_size
    far_stride = TOK_DEV // far_count
    near = [
        pick_rows(member, short_offsets, short_stride)
        for member in (queries, key_rows, value_rows, upstream)
    ]
    near_count = near[0].shape[0]
    segment_keys, segment_values = (
        lax.all_gather(near[1].reshape(near_count, D), "inner", axis=0, tiled=True),
        lax.all_gather(near[2].reshape(near_count, D), "inner", axis=0, tiled=True),
    )
    near_grads = attend_back(near[0], as_heads(segment_keys), as_heads(segment_values), near[3])
    returned = (
        lax.psum_scatter(
            near_grads[1].reshape(KEEP_A, D), "inner", scatter_dimension=0, tiled=True
        ),
        lax.psum_scatter(
            near_grads[2].reshape(KEEP_A, D), "inner", scatter_dimension=0, tiled=True
        ),
    )
    near_final = [near_grads[0], as_heads(returned[0]), as_heads(returned[1])]
    far = [
        pick_rows(member, global_offsets, far_stride).reshape(far_count, D)
        for member in (queries, key_rows, value_rows, upstream)
    ]
    gathered = (
        lax.all_gather(far[0], ("outer", "inner"), axis=0, tiled=True),
        lax.all_gather(far[1], ("outer", "inner"), axis=0, tiled=True),
        lax.all_gather(far[2], ("outer", "inner"), axis=0, tiled=True),
        lax.all_gather(far[3], ("outer", "inner"), axis=0, tiled=True),
    )
    whole_grads = grouped_back(
        as_heads(gathered[0]), as_heads(gathered[1]), as_heads(gathered[2]), as_heads(gathered[3])
    )
    start = lax.axis_index(("outer", "inner")) * far_count
    far_final = [lax.dynamic_slice_in_dim(member, start, far_count, 0) for member in whole_grads]
    results = []
    for index in range(3):
        total = put_rows(near_final[index], short_offsets, short_stride) + put_rows(
            far_final[index], global_offsets, far_stride
        )
        results.append(total.astype(jnp.bfloat16))
    return (results[0], results[1], results[2])


def solution(mesh):
    in_specs = (
        P(("outer", "inner"), None),
        P(("outer", "inner"), None),
        P(("outer", "inner"), None),
        P(("outer", "inner"), None),
        P(),
        P(),
    )
    out_specs = (
        P(("outer", "inner"), None),
        P(("outer", "inner"), None),
        P(("outer", "inner"), None),
    )
    return jax.shard_map(local, mesh=mesh, in_specs=in_specs, out_specs=out_specs, check_vma=False)
```

profile of v0, /device:TPU:32, one launch (start us, length us, event | category | flops | bytes accessed | tf_op | source)
XLA Modules:
  0.0 1869.0 jit_solution(2609448415388892153)
XLA Ops:
  7.9 2.0 reshape.188
  10.8 2.0 reshape.190
  12.8 2.8 reshape.189
  15.6 4.7 multiply_reduce_fusion.4
  20.3 2.3 copy.74
  22.8 2.3 copy.76
  28.5 2.0 reshape.195
  33.9 8.9 multiply_reduce_fusion.6
  42.8 1.8 copy.104
  44.7 1.8 copy.106
  46.5 1.8 copy.107
  49.2 1.5 copy.75
  51.6 4.9 fusion.81
  56.5 2.6 fusion.61
  59.1 22.5 %all-gather.13.cloned.1.call-done = bf16[512,1536]{0,1:T(8,128)(2,1)} async-done(((bf16[128,1536]{0,1:T(8,128)(2,1)}), bf16[512,1536]{0,1:T(8,128)(2,1)}) %all-gather.13.cloned.1.call-update) | async-done | bytes 1572880 | tf_op jit(solution)/shard_map/all_gather | solution.py:93
  81.6 2.3 fusion.64
  83.9 2.8 multiply_convert_fusion.1
  86.7 2.3 convolution_multiply_fusion.2
  89.1 3.7 fusion.62
  92.8 2.5 copy.79
  95.3 2.3 fusion.82
  97.6 405.1 %all-gather.15.cloned.1.call-done = bf16[256,2,1536]{2,1,0:T(2,128)(2,1)} async-done(((bf16[1,2,1536]{2,1,0:T(2,128)(2,1)}), bf16[256,2,1536]{2,1,0:T(2,128)(2,1)}) %all-gather.15.cloned.1.call-update) | async-done | bytes 1572880 | tf_op jit(solution)/shard_map/all_gather | solution.py:111
  502.7 5.2 reshape_reshape.12
  507.9 2.9 copy.88
  510.8 407.4 %all-gather.19.cloned.1.call-done = bf16[256,2,1536]{2,1,0:T(2,128)(2,1)} async-done(((bf16[1,2,1536]{2,1,0:T(2,128)(2,1)}), bf16[256,2,1536]{2,1,0:T(2,128)(2,1)}) %all-gather.19.cloned.1.call-update) | async-done | bytes 1572880 | tf_op jit(solution)/shard_map/all_gather | solution.py:113
  918.2 5.8 reshape_reshape.14
  924.0 2.9 copy.90
  926.9 406.7 %all-gather.21.cloned.1.call-done = bf16[256,2,1536]{2,1,0:T(2,128)(2,1)} async-done(((bf16[1,2,1536]{2,1,0:T(2,128)(2,1)}), bf16[256,2,1536]{2,1,0:T(2,128)(2,1)}) %all-gather.21.cloned.1.call-update) | async-done | bytes 1572880 | tf_op jit(solution)/shard_map/all_gather | solution.py:112
  1333.6 5.8 reshape_reshape.15
  1339.5 4.2 copy.91
  1343.6 406.1 %all-gather.17.cloned.1.call-done = bf16[256,2,1536]{2,1,0:T(2,128)(2,1)} async-done(((bf16[1,2,1536]{2,1,0:T(2,128)(2,1)}), bf16[256,2,1536]{2,1,0:T(2,128)(2,1)}) %all-gather.17.cloned.1.call-update) | async-done | bytes 1572880 | tf_op jit(solution)/shard_map/all_gather | solution.py:110
  1749.7 5.8 reshape_reshape.13
  1755.5 4.3 copy.89
  1759.8 60.5 %while.14 = (s32[]{:T(128)}, f32[4,512,4,96]{1,3,2,0:T(8,128)}, f32[4,512,4,96]{1,3,2,0:T(8,128)}, f32[4,512,4,96]{1,3,2,0:T(8,128)}, bf16[4,512,4,96]{1,3,2,0:T...) while((s32[]{:T(128)}, f32[4,512,4,96]{1,3,2,0:T(8,128)}, ...), condition=%wide.region_15.0_spmd, body=%wide.region_11.15_spmd.sunk | while | flops 1218378240 | bytes 54179996 | solution.py:68
  1759.8 4.7 fusion.131
  1764.4 3.0 fusion.132
  1769.3 1.7 fusion.136
  1771.0 2.7 fusion.135
  1775.0 4.5 fusion.131
  1779.6 3.0 fusion.132
  1784.3 1.6 fusion.136
  1786.0 2.7 fusion.135
  1790.1 4.5 fusion.131
  1794.6 3.0 fusion.132
  1799.3 1.7 fusion.136
  1801.0 2.7 fusion.135
  1805.0 4.5 fusion.131
  1809.5 3.0 fusion.132
  1814.4 1.6 fusion.136
  1816.0 2.7 fusion.135
  1820.2 1.4 constant_dynamic-slice_fusion.2
  1821.7 1.9 constant_dynamic-slice_fusion
  1823.5 7.4 broadcast_multiply_fusion.3
  1831.0 1.7 copy.98
  1832.7 1.5 copy.115
  1834.2 1.6 copy.95
  1835.9 1.6 copy.92
  1837.6 2.6 copy.94
  1840.2 2.5 copy.97
  1842.7 4.6 broadcast_multiply_fusion
  1847.3 3.1 mul.247
  1850.4 3.1 mul.240
  1853.5 2.2 mul.222
  1855.6 3.1 add_convert_fusion
  (102 shorter events, 26.5 us)
Async XLA Ops:
  7.2 2.8 copy-start.10
  7.2 44.5 %all-gather.11.cloned.1.call-start = ((), (), s32[]{:S(2)}) async-start(), calls=%async_computation.2 | async-start | bytes 1966080 | tf_op jit(solution)/shard_map/all_gather | solution.py:92
  20.3 5.2 copy-start.9
  20.3 6.4 copy-start.11
  22.7 58.9 %all-gather.13.cloned.1.call-start = ((), (), s32[]{:S(2)}) async-start(), calls=%async_computation.3 | async-start | bytes 1966080 | tf_op jit(solution)/shard_map/all_gather | solution.py:93
  22.7 5.2 copy-start.12
  25.0 3.1 copy-start.13
  25.1 477.6 %all-gather.15.cloned.1.call-start = ((), (), s32[]{:S(2)}) async-start(), calls=%async_computation.6 | async-start | bytes 1579008 | tf_op jit(solution)/shard_map/all_gather | solution.py:111
  28.2 2.3 copy-start.14
  30.5 3.2 copy-start.19
  31.6 2.2 copy-start.15
  32.6 1.3 copy-start.16
  42.8 7.9 copy-start.17
  44.6 873.5 %all-gather.19.cloned.1.call-start = ((), (), s32[]{:S(2)}) async-start(), calls=%async_computation.8 | async-start | bytes 1579008 | tf_op jit(solution)/shard_map/all_gather | solution.py:113
  46.5 1287.1 %all-gather.21.cloned.1.call-start = ((), (), s32[]{:S(2)}) async-start(), calls=%async_computation.9 | async-start | bytes 1579008 | tf_op jit(solution)/shard_map/all_gather | solution.py:112
  48.3 1701.3 %all-gather.17.cloned.1.call-start = ((), (), s32[]{:S(2)}) async-start(), calls=%async_computation.7 | async-start | bytes 1579008 | tf_op jit(solution)/shard_map/all_gather | solution.py:110
  49.2 1788.4 %reduce-scatter.3.cloned.1.call-start = ((), (), s32[]{:S(2)}) async-start(), calls=%async_computation.4 | async-start | bytes 3932160 | tf_op jit(solution)/shard_map/reduce_scatter | solution.py:97
  81.6 2.3 copy-start.18
  86.7 2.3 copy-start.1
  89.0 1751.2 %reduce-scatter.5.cloned.1.call-start = ((), (), s32[]{:S(2)}) async-start(), calls=%async_computation.5 | async-start | bytes 3932160 | tf_op jit(solution)/shard_map/reduce_scatter | solution.py:100
  1755.5 4.3 copy-start.2
  1764.4 3.0 copy-start.3
  1764.4 4.1 copy-start
  1779.6 3.0 copy-start.3
  1779.6 4.0 copy-start
  1794.6 3.0 copy-start.3
  1794.6 3.9 copy-start
  1809.5 3.0 copy-start.3
  1809.5 4.1 copy-start
  1837.6 5.1 copy-start.8
  1855.6 3.1 copy-start.4
  1855.6 3.1 copy-start.6
  1858.7 1.7 copy-start.5
  1858.7 2.2 copy-start.7
Sparse Core Ops, SparseCore 0:
  22.8 28.7 all-gather.10
  53.4 28.0 all-gather.12
  84.0 418.6 all-gather.14
  504.4 413.6 all-gather.18
  919.9 413.6 all-gather.20
  1335.9 413.6 all-gather.16
  1752.2 36.1 reduce-scatter.2
  1791.0 40.2 reduce-scatter.4
where the time goes:
time: 1880 us; the launch traced here: 1870 us
  waiting for transfers between devices  1650 us (88%)
  local copies, waits for them, and re-layouts  94.6 us (5%)
  matrix products  64.3 us (3%)
  other arithmetic  46.1 us (2%)
    all_gather x1, waiting for transfers between devices, local(): lax.all_gather(far[3], ('outer', 'inner'), axis=0, tiled=True)  407 us
    all_gather x1, waiting for transfers between devices, local(): lax.all_gather(far[2], ('outer', 'inner'), axis=0, tiled=True)  407 us
    all_gather x1, waiting for transfers between devices, local(): lax.all_gather(far[0], ('outer', 'inner'), axis=0, tiled=True)  406 us
    all_gather x1, waiting for transfers between devices, local(): lax.all_gather(far[1], ('outer', 'inner'), axis=0, tiled=True)  405 us
  transfers between devices with their start and end apart: 8, of which 6 were waited for; matrix products, arithmetic and copies ran while one was open for 9% of the time, Pallas kernels for 0%

commit v1 on v0

v1 whole, which is shorter than its diff:
```python
import jax
import jax.numpy as jnp
from jax import lax
from jax.experimental import pallas as pl
from jax.experimental.pallas import tpu as pltpu
from jax.sharding import Mesh
from jax.sharding import PartitionSpec as P


H = 16
HD = 96
D = 1536
TOK = 256
NEAR = 128
FAR_STRIDE = 128
GROUP = 4
LANES = GROUP * HD
INNER = 4
SCALE = HD ** -0.5
LOG2E = 1.4426950408889634

ALL_AXES = ("xh", "zh", "zl", "y", "xl", "c")
SIZES = (2, 2, 4, 4, 2, 2)
PAIR = ("xl", "c")
CORE_GROUPS = [[2 * chip + core for chip in range(127, -1, -1)] for core in range(2)]
HEAD_GROUPS = [[64 * r + 4 * h + rest for h in range(15, -1, -1)] for r in range(4) for rest in range(4)]


def nn(a, b):
    return lax.dot_general(a, b, (((1,), (0,)), ((), ())), preferred_element_type=jnp.float32)


def nt(a, b):
    return lax.dot_general(a, b, (((1,), (1,)), ((), ())), preferred_element_type=jnp.float32)


def tn(a, b):
    return lax.dot_general(a, b, (((0,), (0,)), ((), ())), preferred_element_type=jnp.float32)


def lane_of_heads(values, shape):
    lane = lax.broadcasted_iota(jnp.int32, shape, len(shape) - 1)
    spread = jnp.full(shape, values[-1], jnp.int32)
    for hl in range(len(values) - 2, -1, -1):
        spread = jnp.where(lane < (hl + 1) * HD, values[hl], spread)
    return spread


RESIDENT = pl.BlockSpec(memory_space=pltpu.VMEM)


def resident(shape, dtype):
    return pltpu.VMEM(shape, dtype)


GRANT = pltpu.CompilerParams(vmem_limit_bytes=20 * 2**20)


def in_hbm(xs):
    return [pltpu.with_memory_space_constraint(x, pltpu.HBM) for x in xs]


def kept(xs):
    return [pltpu.with_memory_space_constraint(x, pltpu.VMEM) for x in xs]


SCALARS = pl.BlockSpec(memory_space=pltpu.SMEM)
REMAIN = pl.BlockSpec(memory_space=pltpu.HBM)


def pick_kernel(so, go, q_ref, k_ref, v_ref, g_ref, *outs):
    near_refs, (far_ref, blocks, near, selector, rows, low, in_sems, sems) = outs[:INNER], outs[INNER:]
    loads = []
    for t, ref in enumerate((q_ref, k_ref, v_ref, g_ref)):
        for half in range(2):
            part = pl.ds(half * NEAR, NEAR)
            loads.append(pltpu.make_async_copy(ref.at[part], blocks.at[t, part], in_sems.at[2 * t + half]))
    for load in loads:
        load.start()
    me = lax.axis_index(PAIR)
    row = lax.broadcasted_iota(jnp.int32, (2 * NEAR, TOK), 0)
    col = lax.broadcasted_iota(jnp.int32, (2 * NEAR, TOK), 1)
    target = jnp.where(row < NEAR, 2 * row, 2 * (row - NEAR) + 1)
    selector[: 2 * NEAR, :] = (col == target).astype(jnp.bfloat16)
    frow = lax.broadcasted_iota(jnp.int32, (2 * H, TOK), 0)
    fcol = lax.broadcasted_iota(jnp.int32, (2 * H, TOK), 1)
    ftarget = jnp.zeros((2 * H, TOK), jnp.int32)
    for h in range(H):
        ftarget = jnp.where(frow >= 2 * h, go[h], ftarget)
    ftarget = ftarget + FAR_STRIDE * (frow & 1)
    selector[2 * NEAR :, :] = (fcol == ftarget).astype(jnp.bfloat16)
    fars = []
    for t in range(4):
        loads[2 * t].wait()
        loads[2 * t + 1].wait()
        for g in range(INNER):
            lanes = slice(g * LANES, (g + 1) * LANES)
            odd = lane_of_heads([so[g * GROUP + hl] for hl in range(GROUP)], (1, LANES)) == 1
            both = nn(selector[...], blocks[t, :, lanes])
            near[t, :, lanes] = jnp.where(odd, both[NEAR : 2 * NEAR], both[:NEAR]).astype(jnp.bfloat16)
            fars.append(both[2 * NEAR + 8 * g : 2 * NEAR + 8 * (g + 1)])
    for h in range(H):
        g, hl = divmod(h, GROUP)
        for j in range(2):
            line = [fars[t * INNER + g][2 * hl + j : 2 * hl + j + 1, hl * HD : (hl + 1) * HD] for t in range(4)]
            line = jnp.concatenate(line, axis=1)
            for xl in range(2):
                rows[2 * (H - 1 - h) + xl, j : j + 1, :] = line
    low[...] = rows[...].astype(jnp.bfloat16)
    copies = [pltpu.make_async_copy(low, far_ref.at[pl.ds(r * 2 * H, 2 * H)], sems.at[r]) for r in range(4)]
    for copy in copies:
        copy.start()
    for m in range(INNER):
        lanes = pl.ds(pl.multiple_of((me ^ m) * LANES, LANES), LANES)
        for t in range(4):
            near_refs[m][:, t * LANES : (t + 1) * LANES] = near[t, :, lanes]
    for copy in copies:
        copy.wait()


def pick(so, go, members):
    return pl.pallas_call(
        pick_kernel,
        in_specs=[SCALARS] * 2 + [REMAIN] * 4,
        out_specs=[RESIDENT] * INNER + [REMAIN],
        scratch_shapes=[
            pltpu.VMEM((4, TOK, D), jnp.bfloat16),
            pltpu.VMEM((4, NEAR, D), jnp.bfloat16),
            pltpu.VMEM((2 * NEAR + 2 * H, TOK), jnp.bfloat16),
            pltpu.VMEM((2 * H, 2, LANES), jnp.float32),
            pltpu.VMEM((2 * H, 2, LANES), jnp.bfloat16),
            pltpu.SemaphoreType.DMA((8,)),
            pltpu.SemaphoreType.DMA((4,)),
        ],
        out_shape=[resident((NEAR, 4 * LANES), jnp.bfloat16)] * INNER + [pltpu.HBM((128, 2, LANES), jnp.bfloat16)],
        compiler_params=GRANT,
        name="pick",
    )(*in_hbm([so, go, *members]))


def attend(q, k, v, g):
    scores = nt(k, q)
    top = jnp.max(scores, axis=0, keepdims=True)
    weights = jnp.exp2((scores - top) * (SCALE * LOG2E))
    probs = weights * (1.0 / jnp.sum(weights, axis=0, keepdims=True))
    low = probs.astype(jnp.bfloat16)
    dprobs = nt(v, g)
    delta = jnp.sum(low.astype(jnp.float32) * dprobs, axis=0, keepdims=True)
    dscores = (probs * (dprobs - delta)).astype(jnp.bfloat16)
    return tn(k, dscores).T * SCALE, nn(dscores, q) * SCALE, nn(low, g)


def near_kernel(*refs):
    ins, outs = refs[:INNER], refs[INNER:]
    for hl in range(GROUP):
        parts = []
        for t in range(4):
            lo = t * LANES + hl * HD
            parts.append(jnp.concatenate([ref[:, lo : lo + HD] for ref in ins], axis=0))
        for a, grad in enumerate(attend(*parts)):
            low = grad.astype(jnp.bfloat16)
            lo = a * LANES + hl * HD
            for m, out in enumerate(outs):
                out[:, lo : lo + HD] = low[m * NEAR : (m + 1) * NEAR]


def near_back(blocks):
    return pl.pallas_call(
        near_kernel,
        in_specs=[RESIDENT] * INNER,
        out_specs=[RESIDENT] * INNER,
        out_shape=[resident((NEAR, 3 * LANES), jnp.bfloat16)] * INNER,
        compiler_params=GRANT,
        name="near_back",
    )(*kept(blocks))


def far_kernel(own_ref, other_ref, out_ref, grads_ref):
    rows = jnp.concatenate([ref[...].reshape(256, LANES) for ref in (own_ref, other_ref)], axis=0)
    grads = attend(*[rows[:, t * HD : (t + 1) * HD] for t in range(4)])
    first = (3 - lax.axis_index(("xh", "zh"))) * 64 + 2 - 2 * lax.axis_index("xl")
    for a in range(3):
        grads_ref[a] = grads[a]
    for a in range(3):
        for j in range(2):
            out_ref[:, 2 * a + j, :] = grads_ref[a, pl.ds(first + j, 16, stride=4), :]
    out_ref[:, 6, :] = jnp.zeros((16, HD), jnp.float32)
    out_ref[:, 7, :] = jnp.zeros((16, HD), jnp.float32)


def far_back(halves):
    return pl.pallas_call(
        far_kernel,
        in_specs=[RESIDENT] * 2,
        out_specs=RESIDENT,
        scratch_shapes=[pltpu.VMEM((3, 512, HD), jnp.float32)],
        out_shape=resident((16, 8, HD), jnp.float32),
        compiler_params=GRANT,
        name="far_back",
    )(*kept(halves))


def spread_kernel(so, *refs):
    near_refs, outs = refs[:INNER], refs[INNER:]
    me = lax.axis_index(PAIR)
    row = lax.broadcasted_iota(jnp.int32, (TOK, 2 * NEAR), 0)
    col = lax.broadcasted_iota(jnp.int32, (TOK, 2 * NEAR), 1)
    target = jnp.where(col < NEAR, 2 * col, 2 * (col - NEAR) + 1)
    spread = (row == target).astype(jnp.bfloat16)
    for m in range(INNER):
        group = me ^ m
        odd = lane_of_heads([so[group * GROUP + hl] for hl in range(GROUP)], (1, LANES)) == 1
        lanes = pl.ds(pl.multiple_of(group * LANES, LANES), LANES)
        for a, out in enumerate(outs):
            rows = near_refs[m][:, a * LANES : (a + 1) * LANES]
            zero = jnp.zeros_like(rows)
            stacked = jnp.concatenate([jnp.where(odd, zero, rows), jnp.where(odd, rows, zero)], axis=0)
            out[:, lanes] = nn(spread, stacked).astype(jnp.bfloat16)


def spread_rows(so, near):
    return pl.pallas_call(
        spread_kernel,
        in_specs=[SCALARS] + [RESIDENT] * INNER,
        out_specs=[RESIDENT] * 3,
        out_shape=[resident((TOK, D), jnp.bfloat16)] * 3,
        compiler_params=GRANT,
        name="spread",
    )(*in_hbm([so]), *kept(near))


def finish_kernel(go, n0, n1, n2, far_ref, *rest):
    outs, (stage, sems) = rest[:3], rest[3:]
    stores = []
    for a, (near, out) in enumerate(zip((n0, n1, n2), outs)):
        for j in range(2):
            part = slice(j * FAR_STRIDE, (j + 1) * FAR_STRIDE)
            for g in range(INNER):
                lanes = slice(g * LANES, (g + 1) * LANES)
                spot = lane_of_heads([go[g * GROUP + hl] for hl in range(GROUP)], (1, LANES))
                here = lax.broadcasted_iota(jnp.int32, (FAR_STRIDE, LANES), 0) == spot
                line = jnp.concatenate(
                    [far_ref[H - 1 - g * GROUP - hl, 2 * a + j : 2 * a + j + 1, :] for hl in range(GROUP)], axis=1
                )
                total = near[part, lanes].astype(jnp.float32) + jnp.where(here, line, 0.0)
                stage[a, part, lanes] = total.astype(jnp.bfloat16)
            store = pltpu.make_async_copy(stage.at[a, part], out.at[part], sems.at[2 * a + j])
            store.start()
            stores.append(store)
    for store in stores:
        store.wait()


def finish(go, near, far):
    return pl.pallas_call(
        finish_kernel,
        in_specs=[SCALARS] + [RESIDENT] * 4,
        out_specs=[REMAIN] * 3,
        scratch_shapes=[pltpu.VMEM((3, TOK, D), jnp.bfloat16), pltpu.SemaphoreType.DMA((6,))],
        out_shape=[pltpu.HBM((TOK, D), jnp.bfloat16)] * 3,
        compiler_params=GRANT,
        name="finish",
    )(*in_hbm([go]), *kept([*near, far]))


def swap(x, m):
    return lax.ppermute(x, PAIR, [(i, i ^ m) for i in range(INNER)])


def exchange(blocks):
    out = [blocks[0]]
    for m in range(1, INNER):
        out.append(swap(blocks[m], m))
    return out


def local(queries, key_rows, value_rows, upstream, short_offsets, global_offsets):
    *mine, far_out = pick(short_offsets, global_offsets, (queries, key_rows, value_rows, upstream))
    blocks = exchange(mine)
    far = lax.all_to_all(far_out, ALL_AXES, 0, 0, axis_index_groups=CORE_GROUPS, tiled=True)
    other = lax.ppermute(far, "c", [(0, 1), (1, 0)])
    near = exchange(near_back(blocks))
    far = far_back([far, other])
    far = lax.all_to_all(far, ALL_AXES, 0, 0, axis_index_groups=HEAD_GROUPS, tiled=True)
    return tuple(finish(global_offsets, spread_rows(short_offsets, near), far))


def solution(mesh):
    split = Mesh(mesh.devices.reshape(SIZES), ALL_AXES)
    rows = P(ALL_AXES, None)
    return jax.shard_map(
        local, mesh=split, in_specs=(rows,) * 4 + (P(), P()), out_specs=(rows,) * 3, check_vma=False
    )
```

time: 1880 us -> 56.7 us (0.03)
  the two profiles are of different devices: /device:TPU:32 before, /device:TPU:1 now
where the time goes in v1:
time: 56.7 us; the launch traced here: 56.5 us
  starting transfers between devices  32.1 us (57%)
  Pallas kernels  16.7 us (29%)
  waiting for transfers between devices  6.88 us (12%)
  between operations  0.86 us (2%)
    all_to_all x1, starting transfers between devices, local(): lax.all_to_all(far_out, ALL_AXES, 0, 0, axis_index_groups=CORE_GROUPS, ti...  15 us
    all_to_all x1, starting transfers between devices, local(): lax.all_to_all(far, ALL_AXES, 0, 0, axis_index_groups=HEAD_GROUPS, tiled=...  9.91 us
    ppermute x6, starting transfers between devices, swap(): return lax.ppermute(x, PAIR, [(i, i ^ m) for i in range(INNER)])  7.16 us
    pallas_call x1, Pallas kernels, near_back(): pl.pallas_call(near_kernel, in_specs=[RESIDENT] * INNER, out_specs=[RESID...  5.46 us
    pallas_call x1, Pallas kernels, pick(): pl.pallas_call(pick_kernel, in_specs=[SCALARS] * 2 + [REMAIN] * 4, out_sp...  4.69 us
    ppermute x6, waiting for transfers between devices, swap(): return lax.ppermute(x, PAIR, [(i, i ^ m) for i in range(INNER)])  3.93 us
    pallas_call x1, Pallas kernels, finish(): pl.pallas_call(finish_kernel, in_specs=[SCALARS] + [RESIDENT] * 4, out_sp...  2.81 us
    pallas_call x1, Pallas kernels, far_back(): pl.pallas_call(far_kernel, in_specs=[RESIDENT] * 2, out_specs=RESIDENT, s...  2.05 us
  transfers between devices with their start and end apart: 9, of which 3 were waited for; matrix products, arithmetic and copies ran while one was open for 0% of the time, Pallas kernels for 16%

profile of v1, /device:TPU:1, one launch (start us, length us, event | category | flops | bytes accessed | tf_op | source)
XLA Modules:
  0.0 56.5 jit_solution(564978414350933963)
XLA Ops:
  0.6 4.7 %pick.1 = (bf16[128,1536]{1,0:T(8,128)(2,1)S(1)}, bf16[128,1536]{1,0:T(8,128)(2,1)S(1)}, bf16[128,1536]{1,0:T(8,128)(2,1)S(1)}, bf16[128,1536]{1,0:T(8,128)(2,1)S(1)}, bf16[128,2,384]{2,1,0:T(2,128)(2,1)}) custom-call(s32[16]{0:T(128)} %so.3, s32[16]{0:T(128)} %go.3, bf16[256,1536]{1,0:T(8,128)(2,1)} %q_ref.1, bf16[256,1536]{1,0:T(8,128)(2,1)} %k_ref.1, ...), custom_call_target="tpu_custom_call" | custom-call | tf_op jit(solution)/shard_map/pick/pallas_call | solution.py:122
  5.3 3.3 %collective-permute-start = (bf16[128,1536]{1,0:T(8,128)(2,1)S(1)}, bf16[128,1536]{1,0:T(8,128)(2,1)S(1)}, u32[]{:S(2)}, u32[]{:S(2)}) collective-permute-start(bf16[128,1536]{1,0:T(8,128)(2,1)S(1)} %get-tuple-element.16), channel_id=1, source_target_pairs={{0,1},{1,0},{2,3},{3,2},{4,5},{5,4},{6,7},{7,6},{8,9},{9,8},{10,11... | collective-permute-start | bytes 1179656 | tf_op jit(solution)/shard_map/ppermute | solution.py:267
  8.6 0.0 collective-permute-start.1
  8.6 1.7 %collective-permute-start.2 = (bf16[128,1536]{1,0:T(8,128)(2,1)S(1)}, bf16[128,1536]{1,0:T(8,128)(2,1)S(1)}, u32[]{:S(2)}, u32[]{:S(2)}) collective-permute-start(bf16[128,1536]{1,0:T(8,128)(2,1)S(1)} %get-tuple-element.18), channel_id=1, source_target_pairs={{0,3},{1,2},{2,1},{3,0},{4,7},{5,6},{6,5},{7,4},{8,11},{9,10},{10,... | collective-permute-start | bytes 1179656 | tf_op jit(solution)/shard_map/ppermute | solution.py:267
  10.3 15.0 %all-to-all-start = ((bf16[128,2,384]{2,1,0:T(2,128)(2,1)}), bf16[128,2,384]{2,1,0:T(2,128)(2,1)S(1)}, u32[]{:S(2)}, u32[]{:S(2)}) async-start(bf16[128,2,384]{2,1,0:T(2,128)(2,1)} %get-tuple-element.26), calls=%async_computation | async-start | bytes 393216 | tf_op jit(solution)/shard_map/all_to_all | solution.py:280
  25.4 0.0 collective-permute-done.refs_1_
  25.4 0.0 collective-permute-done.1.refs_2_
  25.4 3.9 %collective-permute-done.2.refs_3_ = bf16[128,1536]{1,0:T(8,128)(2,1)S(1)} collective-permute-done((bf16[128,1536]{1,0:T(8,128)(2,1)S(1)}, bf16[128,1536]{1,0:T(8,128)(2,1)S(1)}, u32[]{:S(2)}, u32[]{:S(2)}) %collective-permute-start.2) | collective-permute-done | bytes 393248 | tf_op jit(solution)/shard_map/ppermute | solution.py:267
  29.3 5.5 %near_back.1 = (bf16[128,1152]{1,0:T(8,128)(2,1)S(1)}, bf16[128,1152]{1,0:T(8,128)(2,1)}, bf16[128,1152]{1,0:T(8,128)(2,1)S(1)}, bf16[128,1152]{1,0:T(8,128)(2,1)S(1)}) custom-call(bf16[128,1536]{1,0:T(8,128)(2,1)S(1)} %get-tuple-element.15.refs_0_, bf16[128,1536]{1,0:T(8,128)(2,1)S(1)} %collective-permute-done.refs_1_, ...), custom_call_target="tpu_custom_call" | custom-call | tf_op jit(solution)/shard_map/near_back/pallas_call | solution.py:168
  34.8 0.0 collective-permute-start.3
  34.8 0.0 collective-permute-start.4
  34.8 2.1 %collective-permute-start.5 = (bf16[128,1152]{1,0:T(8,128)(2,1)S(1)}, bf16[128,1152]{1,0:T(8,128)(2,1)S(1)}, u32[]{:S(2)}, u32[]{:S(2)}) collective-permute-start(bf16[128,1152]{1,0:T(8,128)(2,1)S(1)} %get-tuple-element.22), channel_id=1, source_target_pairs={{0,3},{1,2},{2,1},{3,0},{4,7},{5,6},{6,5},{7,4},{8,11},{9,10},{10,... | collective-permute-start | bytes 884744 | tf_op jit(solution)/shard_map/ppermute | solution.py:267
  36.9 0.0 all-to-all-done.own_ref
  36.9 0.0 collective-permute-start.6
  36.9 1.4 %collective-permute-done.6.other_ref = bf16[128,2,384]{2,1,0:T(2,128)(2,1)S(1)} collective-permute-done((bf16[128,2,384]{2,1,0:T(2,128)(2,1)S(1)}, bf16[128,2,384]{2,1,0:T(2,128)(2,1)S(1)}, u32[]{:S(2)}, u32[]{:S(2)}) %collective-permute-start.6) | collective-permute-done | bytes 196640 | tf_op jit(solution)/shard_map/ppermute | solution.py:281
  38.3 2.0 %far_back.1 = f32[16,8,96]{2,1,0:T(8,128)} custom-call(bf16[128,2,384]{2,1,0:T(2,128)(2,1)S(1)} %all-to-all-done.own_ref, bf16[128,2,384]{2,1,0:T(2,128)(2,1)S(1)} %collective-permute-done.6.other_ref), custom_call_target="tpu_custom_call" | custom-call | tf_op jit(solution)/shard_map/far_back/pallas_call | solution.py:192
  40.4 9.9 %all-to-all-start.1 = ((f32[16,8,96]{2,1,0:T(8,128)}), f32[16,8,96]{2,1,0:T(8,128)}, u32[]{:S(2)}, u32[]{:S(2)}) async-start(f32[16,8,96]{2,1,0:T(8,128)} %far_back.1), calls=%async_computation.1 | async-start | bytes 131072 | tf_op jit(solution)/shard_map/all_to_all | solution.py:284
  50.3 0.0 collective-permute-done.3.refs_1_
  50.3 0.0 collective-permute-done.4.refs_2_
  50.3 0.0 collective-permute-done.5.refs_3_
  50.3 1.7 %spread.1 = (bf16[256,1536]{1,0:T(8,128)(2,1)S(1)}, bf16[256,1536]{1,0:T(8,128)(2,1)S(1)}, bf16[256,1536]{1,0:T(8,128)(2,1)S(1)}) custom-call(s32[16]{0:T(128)} %so.3, bf16[128,1152]{1,0:T(8,128)(2,1)S(1)} %get-tuple-element.19.refs_0_, bf16[128,1152]{1,0:T(8,128)(2,1)S(1)} %collective-permute-done.3.refs_1_, ...), custom_call_target="tpu_custom_call" | custom-call | tf_op jit(solution)/shard_map/spread/pallas_call | solution.py:222
  52.0 1.5 %all-to-all-done.1.far_ref = f32[16,8,96]{2,1,0:T(8,128)} async-done(((f32[16,8,96]{2,1,0:T(8,128)}), f32[16,8,96]{2,1,0:T(8,128)}, u32[]{:S(2)}, u32[]{:S(2)}) %all-to-all-start.1) | async-done | bytes 49184 | tf_op jit(solution)/shard_map/all_to_all | solution.py:284
  53.5 2.8 %finish.1 = (bf16[256,1536]{1,0:T(8,128)(2,1)}, bf16[256,1536]{1,0:T(8,128)(2,1)}, bf16[256,1536]{1,0:T(8,128)(2,1)}) custom-call(s32[16]{0:T(128)} %go.3, bf16[256,1536]{1,0:T(8,128)(2,1)S(1)} %get-tuple-element.23.n0, bf16[256,1536]{1,0:T(8,128)(2,1)S(1)} %get-tuple-element.24.n1, bf16[256,1536]{1,0:T(8,128)(2,1)S(1)} %get-tuple-element.25.n2, ...), custom_call_target="tpu_custom_call" | custom-call | tf_op jit(solution)/shard_map/finish/pallas_call | solution.py:255
Async XLA Ops:
  5.3 20.0 %collective-permute-start = (bf16[128,1536]{1,0:T(8,128)(2,1)S(1)}, bf16[128,1536]{1,0:T(8,128)(2,1)S(1)}, u32[]{:S(2)}, u32[]{:S(2)}) collective-permute-start(bf16[128,1536]{1,0:T(8,128)(2,1)S(1)} %get-tuple-element.16), channel_id=1, source_target_pairs={{0,1},{1,0},{2,3},{3,2},{4,5},{5,4},{6,7},{7,6},{8,9},{9,8},{10,11... | collective-permute-start | bytes 1179656 | tf_op jit(solution)/shard_map/ppermute | solution.py:267
  8.6 16.8 %collective-permute-start.1 = (bf16[128,1536]{1,0:T(8,128)(2,1)S(1)}, bf16[128,1536]{1,0:T(8,128)(2,1)S(1)}, u32[]{:S(2)}, u32[]{:S(2)}) collective-permute-start(bf16[128,1536]{1,0:T(8,128)(2,1)S(1)} %get-tuple-element.17), channel_id=1, source_target_pairs={{0,2},{1,3},{2,0},{3,1},{4,6},{5,7},{6,4},{7,5},{8,10},{9,11},{10,... | collective-permute-start | bytes 1179656 | tf_op jit(solution)/shard_map/ppermute | solution.py:267
  8.6 20.7 %collective-permute-start.2 = (bf16[128,1536]{1,0:T(8,128)(2,1)S(1)}, bf16[128,1536]{1,0:T(8,128)(2,1)S(1)}, u32[]{:S(2)}, u32[]{:S(2)}) collective-permute-start(bf16[128,1536]{1,0:T(8,128)(2,1)S(1)} %get-tuple-element.18), channel_id=1, source_target_pairs={{0,3},{1,2},{2,1},{3,0},{4,7},{5,6},{6,5},{7,4},{8,11},{9,10},{10,... | collective-permute-start | bytes 1179656 | tf_op jit(solution)/shard_map/ppermute | solution.py:267
  10.3 26.6 %all-to-all-start = ((bf16[128,2,384]{2,1,0:T(2,128)(2,1)}), bf16[128,2,384]{2,1,0:T(2,128)(2,1)S(1)}, u32[]{:S(2)}, u32[]{:S(2)}) async-start(bf16[128,2,384]{2,1,0:T(2,128)(2,1)} %get-tuple-element.26), calls=%async_computation | async-start | bytes 393216 | tf_op jit(solution)/shard_map/all_to_all | solution.py:280
  34.8 15.5 %collective-permute-start.3 = (bf16[128,1152]{1,0:T(8,128)(2,1)}, bf16[128,1152]{1,0:T(8,128)(2,1)S(1)}, u32[]{:S(2)}, u32[]{:S(2)}) collective-permute-start(bf16[128,1152]{1,0:T(8,128)(2,1)} %get-tuple-element.20), channel_id=1, source_target_pairs={{0,1},{1,0},{2,3},{3,2},{4,5},{5,4},{6,7},{7,6},{8,9},{9,8},{10,11... | collective-permute-start | bytes 884744 | tf_op jit(solution)/shard_map/ppermute | solution.py:267
  34.8 15.6 %collective-permute-start.4 = (bf16[128,1152]{1,0:T(8,128)(2,1)S(1)}, bf16[128,1152]{1,0:T(8,128)(2,1)S(1)}, u32[]{:S(2)}, u32[]{:S(2)}) collective-permute-start(bf16[128,1152]{1,0:T(8,128)(2,1)S(1)} %get-tuple-element.21), channel_id=1, source_target_pairs={{0,2},{1,3},{2,0},{3,1},{4,6},{5,7},{6,4},{7,5},{8,10},{9,11},{10,... | collective-permute-start | bytes 884744 | tf_op jit(solution)/shard_map/ppermute | solution.py:267
  34.8 15.6 %collective-permute-start.5 = (bf16[128,1152]{1,0:T(8,128)(2,1)S(1)}, bf16[128,1152]{1,0:T(8,128)(2,1)S(1)}, u32[]{:S(2)}, u32[]{:S(2)}) collective-permute-start(bf16[128,1152]{1,0:T(8,128)(2,1)S(1)} %get-tuple-element.22), channel_id=1, source_target_pairs={{0,3},{1,2},{2,1},{3,0},{4,7},{5,6},{6,5},{7,4},{8,11},{9,10},{10,... | collective-permute-start | bytes 884744 | tf_op jit(solution)/shard_map/ppermute | solution.py:267
  36.9 1.4 %collective-permute-start.6 = (bf16[128,2,384]{2,1,0:T(2,128)(2,1)S(1)}, bf16[128,2,384]{2,1,0:T(2,128)(2,1)S(1)}, u32[]{:S(2)}, u32[]{:S(2)}) collective-permute-start(bf16[128,2,384]{2,1,0:T(2,128)(2,1)S(1)} %all-to-all-done.own_ref), channel_id=1, source_target_pairs={{0,1},{1,0},{2,3},{3,2},{4,5},{5,4},{6,7},{7,6},{8,9},{9,8},{10,11... | collective-permute-start | bytes 589832 | tf_op jit(solution)/shard_map/ppermute | solution.py:281
  40.4 13.1 %all-to-all-start.1 = ((f32[16,8,96]{2,1,0:T(8,128)}), f32[16,8,96]{2,1,0:T(8,128)}, u32[]{:S(2)}, u32[]{:S(2)}) async-start(f32[16,8,96]{2,1,0:T(8,128)} %far_back.1), calls=%async_computation.1 | async-start | bytes 131072 | tf_op jit(solution)/shard_map/all_to_all | solution.py:284
